TPU v7x, 256 devices: a whole 4x4x8 slice. The times are simulated.
256 devices in a mesh: dp: 32 (over y, x, core), mp: 8 (over z).
Axes of the slice: x: 4, y: 4, z: 8, core: 2. Of those that a mesh axis runs over, the one named last changes fastest.
Arguments:
- tokens: bfloat16 [2, 4096, 4096], P(None, 'dp', 'mp'), may hold values from -6 to 6
- targets: bfloat16 [2, 4096, 4096], P(None, 'dp', 'mp'), may hold values from -6 to 6
- weight: bfloat16 [4096, 4096], P('mp'), may hold values from -0.09375 to 0.09375
- basis: bfloat16 [4096, 512], replicated, may hold values from -0.09375 to 0.09375
- moment1: float32 [8, 512, 512], P('mp', 'dp'), may hold values from -0.06 to 0.06
- moment2: float32 [8, 512, 512], P('mp', 'dp'), may hold values from 1e-05 to 0.001
Outputs:
- new_weight: bfloat16 [4096, 4096], P('mp')
- new_moment1: float32 [8, 512, 512], P('mp', 'dp')
- new_moment2: float32 [8, 512, 512], P('mp', 'dp')
All inputs are finite; a program needn't handle non-finite values.
Results may differ from a plain program's by a relative error of at most 0.009.
Values may be sent and summed in bfloat16 or wider, within the bound.
No kernel may reach another device: no remote copies, remote signals or barrier semaphores. Data moves between devices by JAX's collectives and lax.ppermute only.
A program may use at most 64 MiB of HBM per device.

v0:
```python
import jax
import jax.numpy as jnp
from jax import lax
from jax.sharding import PartitionSpec as P

RATE = 0.02
F32 = jnp.float32
BF16 = jnp.bfloat16


def dot(a, b, dims):
    return lax.dot_general(a, b, (dims, ((), ())), preferred_element_type=F32)


def body(tokens, targets, weight, basis, moment1, moment2):
    n_mp = lax.axis_size("mp")
    n_dp = lax.axis_size("dp")
    j = lax.axis_index("mp")
    core = lax.axis_index("dp") % 2
    chips = n_dp // 2
    steps, toks, width = tokens.shape
    total_tokens = toks * n_dp
    rank = basis.shape[1]
    rows_mp = weight.shape[0]
    rows = rows_mp // n_dp
    groups = [[2 * chip + c for chip in range(chips)] for c in range(2)]

    def ahead(a, k):
        return lax.ppermute(a, "mp", [(i, (i + k) % n_mp) for i in range(n_mp)])

    def other_core(a):
        return lax.ppermute(a, "dp", [(i, i ^ 1) for i in range(n_dp)])

    def exchange(a):
        return lax.all_to_all(a, "dp", split_axis=0, concat_axis=0, tiled=True, axis_index_groups=groups)

    def gather_rows(a):
        mine = exchange(jnp.broadcast_to(a, (chips, *a.shape)))
        other = other_core(mine)
        both = [jnp.where(core == 0, mine, other), jnp.where(core == 0, other, mine)]
        return jnp.stack(both, axis=1).reshape(n_dp * a.shape[0], a.shape[1])

    features = jnp.zeros((steps * toks, n_mp * width), BF16)

    def put(features, chunk, s, k):
        return lax.dynamic_update_slice(features, chunk, (s * toks, ((j - k) % n_mp) * width))

    half = n_mp // 2
    right = lax.optimization_barrier([tokens[s] for s in range(steps)])
    left = list(right)
    for s in range(steps):
        features = put(features, right[s], s, 0)
    for k in range(1, half):
        for s in (1, 0):
            right[s] = ahead(right[s], 1)
            left[s] = ahead(left[s], -1)
            features = put(features, right[s], s, k)
            features = put(features, left[s], s, -k)
    right[1] = ahead(right[1], 1)
    left[0] = ahead(left[0], -1)
    features = put(features, right[1], 1, half)
    features = put(features, left[0], 0, half)
    outputs, reduced = lax.optimization_barrier(
        (dot(features, weight, ((1,), (1,))), dot(features, basis, ((1,), (0,))).astype(BF16))
    )

    reduced = reduced.reshape(steps, toks, rank)
    errors = outputs.astype(BF16).astype(F32) - targets.reshape(steps * toks, rows_mp).astype(F32)
    errors = errors.astype(BF16).reshape(steps, toks, rows_mp)
    pairs = [(errors[0], reduced[0]), (errors[1], reduced[1]), (reduced[1], reduced[1])]
    parts = [dot(a, b, ((0,), (0,))).astype(BF16).reshape(chips, 2, -1, rank) for a, b in pairs]
    parts = jnp.concatenate(parts, axis=2)
    away = other_core(lax.dynamic_index_in_dim(parts, 1 - core, 1, keepdims=False))
    kept = lax.dynamic_index_in_dim(parts, core, 1, keepdims=False)
    sums = exchange((kept.astype(F32) + away.astype(F32)).astype(BF16)).astype(F32).sum(axis=0)
    gram = gather_rows(sums[2 * rows :].astype(BF16))

    def update(first, second, projected):
        first = 0.9 * first + 0.1 * projected
        second = 0.95 * second + 0.05 * projected * projected
        direction = (first / (jnp.sqrt(second) + 1e-08)).astype(BF16)
        return first, second, direction

    first, second, d0 = update(moment1[0], moment2[0], sums[:rows] / total_tokens)
    moved = dot(d0, gram, ((1,), (0,)))
    first, second, d1 = update(first, second, (sums[rows : 2 * rows] - RATE * moved) / total_tokens)
    both = (d0.astype(F32) + d1.astype(F32)).astype(BF16)
    lifted = dot(gather_rows(both), basis, ((1,), (1,)))
    new_weight = (weight.astype(F32) - RATE * lifted).astype(BF16)
    return (new_weight, first[None], second[None])


def solution(mesh):
    in_specs = (
        P(None, "dp", "mp"),
        P(None, "dp", "mp"),
        P("mp", None),
        P(),
        P("mp", "dp", None),
        P("mp", "dp", None),
    )
    out_specs = (P("mp", None), P("mp", "dp", None), P("mp", "dp", None))
    return jax.shard_map(body, mesh=mesh, in_specs=in_specs, out_specs=out_specs, check_vma=False)
```

profile of v0, /device:TPU:1, one launch (start us, length us, event | category | flops | bytes accessed | tf_op | source)
XLA Modules:
  0.0 100.1 jit_solution(16940331964027354849)
XLA Ops:
  0.6 1.0 slice_bitcast_fusion
  1.6 2.5 %collective-permute-start = (bf16[128,512]{1,0:T(8,128)(2,1)S(1)}, bf16[128,512]{1,0:T(8,128)(2,1)S(1)}, u32[]{:S(2)}, u32[]{:S(2)}) collective-permute-start(bf16[128,512]{1,0:T(8,128)(2,1)S(1)} %get-tuple-element.8), channel_id=1, source_target_pairs={{0,1},{1,2},{2,3},{3,4},{4,5},{5,6},{6,7},{7,0},{8,9},{9,10},{10,1... | collective-permute-start | bytes 393224 | tf_op jit(solution)/shard_map/ppermute | solution.py:29
  4.2 4.0 %collective-permute-start.1 = (bf16[128,512]{1,0:T(8,128)(2,1)S(1)}, bf16[128,512]{1,0:T(8,128)(2,1)S(1)}, u32[]{:S(2)}, u32[]{:S(2)}) collective-permute-start(bf16[128,512]{1,0:T(8,128)(2,1)S(1)} %get-tuple-element.8), channel_id=1, source_target_pairs={{0,7},{1,0},{2,1},{3,2},{4,3},{5,4},{6,5},{7,6},{8,15},{9,8},{10,9... | collective-permute-start | bytes 393224 | tf_op jit(solution)/shard_map/ppermute | solution.py:29
  8.2 0.0 collective-permute-start.2
  8.2 2.7 %collective-permute-start.3 = (bf16[128,512]{1,0:T(8,128)(2,1)S(1)}, bf16[128,512]{1,0:T(8,128)(2,1)S(1)}, u32[]{:S(2)}, u32[]{:S(2)}) collective-permute-start(bf16[128,512]{1,0:T(8,128)(2,1)S(1)} %get-tuple-element.7), channel_id=1, source_target_pairs={{0,7},{1,0},{2,1},{3,2},{4,3},{5,4},{6,5},{7,6},{8,15},{9,8},{10,9... | collective-permute-start | bytes 393224 | tf_op jit(solution)/shard_map/ppermute | solution.py:29
  10.9 0.2 broadcast_in_dim.15
  11.3 0.0 collective-permute-done
  11.3 0.1 collective-permute-start.4
  11.4 0.0 collective-permute-done.1
  11.4 2.7 %collective-permute-start.5 = (bf16[128,512]{1,0:T(8,128)(2,1)S(1)}, bf16[128,512]{1,0:T(8,128)(2,1)S(1)}, u32[]{:S(2)}, u32[]{:S(2)}) collective-permute-start(bf16[128,512]{1,0:T(8,128)(2,1)S(1)} %collective-permute-done.1), channel_id=1, source_target_pairs={{0,7},{1,0},{2,1},{3,2},{4,3},{5,4},{6,5},{7,6},{8,15},{9,8},{10,9... | collective-permute-start | bytes 393224 | tf_op jit(solution)/shard_map/ppermute | solution.py:29
  14.1 0.0 collective-permute-done.2
  14.1 0.0 collective-permute-start.6
  14.1 0.0 collective-permute-done.3
  14.1 2.7 %collective-permute-start.7 = (bf16[128,512]{1,0:T(8,128)(2,1)S(1)}, bf16[128,512]{1,0:T(8,128)(2,1)S(1)}, u32[]{:S(2)}, u32[]{:S(2)}) collective-permute-start(bf16[128,512]{1,0:T(8,128)(2,1)S(1)} %collective-permute-done.3), channel_id=1, source_target_pairs={{0,7},{1,0},{2,1},{3,2},{4,3},{5,4},{6,5},{7,6},{8,15},{9,8},{10,9... | collective-permute-start | bytes 393224 | tf_op jit(solution)/shard_map/ppermute | solution.py:29
  16.8 0.0 collective-permute-done.4
  16.8 0.1 collective-permute-start.8
  16.9 0.0 collective-permute-done.5
  16.9 2.7 %collective-permute-start.9 = (bf16[128,512]{1,0:T(8,128)(2,1)S(1)}, bf16[128,512]{1,0:T(8,128)(2,1)S(1)}, u32[]{:S(2)}, u32[]{:S(2)}) collective-permute-start(bf16[128,512]{1,0:T(8,128)(2,1)S(1)} %collective-permute-done.5), channel_id=1, source_target_pairs={{0,7},{1,0},{2,1},{3,2},{4,3},{5,4},{6,5},{7,6},{8,15},{9,8},{10,9... | collective-permute-start | bytes 393224 | tf_op jit(solution)/shard_map/ppermute | solution.py:29
  19.6 0.2 collective-permute-done.6
  19.8 0.0 collective-permute-start.10
  19.8 0.0 collective-permute-done.7
  19.8 3.0 %collective-permute-start.11 = (bf16[128,512]{1,0:T(8,128)(2,1)S(1)}, bf16[128,512]{1,0:T(8,128)(2,1)S(1)}, u32[]{:S(2)}, u32[]{:S(2)}) collective-permute-start(bf16[128,512]{1,0:T(8,128)(2,1)S(1)} %collective-permute-done.7), channel_id=1, source_target_pairs={{0,7},{1,0},{2,1},{3,2},{4,3},{5,4},{6,5},{7,6},{8,15},{9,8},{10,9... | collective-permute-start | bytes 393224 | tf_op jit(solution)/shard_map/ppermute | solution.py:29
  22.8 0.2 collective-permute-done.8
  23.0 0.0 collective-permute-start.12
  23.0 2.3 %collective-permute-done.11 = bf16[128,512]{1,0:T(8,128)(2,1)S(1)} collective-permute-done((bf16[128,512]{1,0:T(8,128)(2,1)S(1)}, bf16[128,512]{1,0:T(8,128)(2,1)S(1)}, u32[]{:S(2)}, u32[]{:S(2)}) %collective-permute-start.11) | collective-permute-done | bytes 131104 | tf_op jit(solution)/shard_map/ppermute | solution.py:29
  25.3 3.4 %collective-permute-start.13 = (bf16[128,512]{1,0:T(8,128)(2,1)S(1)}, bf16[128,512]{1,0:T(8,128)(2,1)S(1)}, u32[]{:S(2)}, u32[]{:S(2)}) collective-permute-start(bf16[128,512]{1,0:T(8,128)(2,1)S(1)} %collective-permute-done.11), channel_id=1, source_target_pairs={{0,7},{1,0},{2,1},{3,2},{4,3},{5,4},{6,5},{7,6},{8,15},{9,8},{10,9... | collective-permute-start | bytes 393224 | tf_op jit(solution)/shard_map/ppermute | solution.py:29
  28.8 0.0 collective-permute-done.9
  28.8 0.0 collective-permute-done.10
  28.9 0.1 collective-permute-done.12
  28.9 1.8 %collective-permute-done.13 = bf16[128,512]{1,0:T(8,128)(2,1)S(1)} collective-permute-done((bf16[128,512]{1,0:T(8,128)(2,1)S(1)}, bf16[128,512]{1,0:T(8,128)(2,1)S(1)}, u32[]{:S(2)}, u32[]{:S(2)}) %collective-permute-start.13) | collective-permute-done | bytes 131104 | tf_op jit(solution)/shard_map/ppermute | solution.py:29
  30.7 0.0 copy-start.1
  30.7 3.6 %convolution_convert_fusion.3 = bf16[256,512]{1,0:T(8,128)(2,1)S(1)} fusion(bf16[256,4096]{1,0:T(8,128)(2,1)S(1)} %constant_dynamic-update-slice_fusion, bf16[4096,512]{1,0:T(8,128)(2,1)} %param.9), kind=kOutput, calls=%fused_computation.8 | convolution fusion | flops 1073872896 | bytes 6553600 | tf_op jit(solution)/shard_map/dot_general | solution.py:12
  34.3 0.0 copy-done.1
  34.3 0.0 copy-start
  34.3 1.3 %fusion.9 = bf16[256,512]{1,0:T(8,128)(2,1)S(1)} fusion(bf16[256,4096]{1,0:T(8,128)(2,1)S(1)} %constant_dynamic-update-slice_fusion, bf16[512,4096]{1,0:T(8,128)(2,1)S(1)} %copy-done.1), kind=kOutput, calls=%fused_computation.53 | convolution fusion | flops 1073741824 | bytes 6553600 | tf_op jit(solution)/shard_map/dot_general | solution.py:12
  35.6 0.0 copy-done
  35.6 0.1 fusion.1
  35.7 0.3 convolution_convert_fusion.2
  36.0 0.3 convolution_convert_fusion.1
  36.4 0.3 convolution_convert_fusion
  36.7 0.1 pad_maximum_fusion
  36.8 0.1 dynamic-slice_bitcast_fusion
  36.9 5.0 %collective-permute-start.14 = (bf16[16,48,512]{2,1,0:T(8,128)(2,1)S(1)}, bf16[16,48,512]{2,1,0:T(8,128)(2,1)S(1)}, u32[]{:S(2)}, u32[]{:S(2)}) collective-permute-start(bf16[16,48,512]{2,1,0:T(8,128)(2,1)S(1)} %dynamic-slice_bitcast_fusion), channel_id=1, source_target_pairs={{0,8},{8,0},{16,24},{24,16},{32,40},{40,32},{48,56},{56,48},{64,72... | collective-permute-start | bytes 2359304 | tf_op jit(solution)/shard_map/ppermute | solution.py:32
  41.9 1.9 %collective-permute-done.14 = bf16[16,48,512]{2,1,0:T(8,128)(2,1)S(1)} collective-permute-done((bf16[16,48,512]{2,1,0:T(8,128)(2,1)S(1)}, bf16[16,48,512]{2,1,0:T(8,128)(2,1)S(1)}, u32[]{:S(2)}, u32[]{:S(2)}) %collective-permute-start.14) | collective-permute-done | bytes 786464 | tf_op jit(solution)/shard_map/ppermute | solution.py:32
  43.8 0.2 fusion
  44.1 20.4 %all_to_all.15 = bf16[16,48,512]{2,1,0:T(8,128)(2,1)S(1)} all-to-all(bf16[16,48,512]{2,1,0:T(8,128)(2,1)S(1)} %fusion), channel_id=1, replica_groups={{0,16,32,48,64,80,96,112,128,144,160,176,192,208,224,240},{8,24,40,56,7..., dimensions={0} | all-to-all | bytes 1572864 | tf_op jit(solution)/shard_map/all_to_all | solution.py:35
  64.5 0.0 copy-start.3
  64.5 0.0 copy-start.4
  64.5 0.1 convert_reduce_fusion
  64.6 10.8 %all_to_all.16 = bf16[16,16,512]{2,1,0:T(8,128)(2,1)S(1)} all-to-all(bf16[16,16,512]{2,1,0:T(8,128)(2,1)S(1)} %broadcast_in_dim.16), channel_id=1, replica_groups={{0,16,32,48,64,80,96,112,128,144,160,176,192,208,224,240},{8,24,40,56,7..., dimensions={0} | all-to-all | bytes 524288 | tf_op jit(solution)/shard_map/all_to_all | solution.py:35
  75.4 2.3 %collective-permute-start.15 = (bf16[16,16,512]{2,1,0:T(8,128)(2,1)S(1)}, bf16[16,16,512]{2,1,0:T(8,128)(2,1)S(1)}, u32[]{:S(2)}, u32[]{:S(2)}) collective-permute-start(bf16[16,16,512]{2,1,0:T(8,128)(2,1)S(1)} %all_to_all.16), channel_id=1, source_target_pairs={{0,8},{8,0},{16,24},{24,16},{32,40},{40,32},{48,56},{56,48},{64,72... | collective-permute-start | bytes 786440 | tf_op jit(solution)/shard_map/ppermute | solution.py:32
  77.7 1.2 %collective-permute-done.15 = bf16[16,16,512]{2,1,0:T(8,128)(2,1)S(1)} collective-permute-done((bf16[16,16,512]{2,1,0:T(8,128)(2,1)S(1)}, bf16[16,16,512]{2,1,0:T(8,128)(2,1)S(1)}, u32[]{:S(2)}, u32[]{:S(2)}) %collective-permute-start.15) | collective-permute-done | bytes 262176 | tf_op jit(solution)/shard_map/ppermute | solution.py:32
  78.9 0.1 pad_maximum_fusion.1
  78.9 0.0 copy-done.3
  79.0 0.0 copy-done.4
  79.0 0.0 copy-start.2
  79.0 0.8 fusion.8
  79.8 10.9 %all_to_all.17 = bf16[16,16,512]{2,1,0:T(8,128)(2,1)S(1)} all-to-all(bf16[16,16,512]{2,1,0:T(8,128)(2,1)S(1)} %broadcast_in_dim.17), channel_id=1, replica_groups={{0,16,32,48,64,80,96,112,128,144,160,176,192,208,224,240},{8,24,40,56,7..., dimensions={0} | all-to-all | bytes 524288 | tf_op jit(solution)/shard_map/all_to_all | solution.py:35
  90.7 1.5 %collective-permute-start.16 = (bf16[16,16,512]{2,1,0:T(8,128)(2,1)S(1)}, bf16[16,16,512]{2,1,0:T(8,128)(2,1)S(1)}, u32[]{:S(2)}, u32[]{:S(2)}) collective-permute-start(bf16[16,16,512]{2,1,0:T(8,128)(2,1)S(1)} %all_to_all.17), channel_id=1, source_target_pairs={{0,8},{8,0},{16,24},{24,16},{32,40},{40,32},{48,56},{56,48},{64,72... | collective-permute-start | bytes 786440 | tf_op jit(solution)/shard_map/ppermute | solution.py:32
  92.2 1.2 %collective-permute-done.16 = bf16[16,16,512]{2,1,0:T(8,128)(2,1)S(1)} collective-permute-done((bf16[16,16,512]{2,1,0:T(8,128)(2,1)S(1)}, bf16[16,16,512]{2,1,0:T(8,128)(2,1)S(1)}, u32[]{:S(2)}, u32[]{:S(2)}) %collective-permute-start.16) | collective-permute-done | bytes 262176 | tf_op jit(solution)/shard_map/ppermute | solution.py:32
  93.4 0.1 pad_maximum_fusion.2
  93.5 0.0 copy-done.2
  93.5 6.6 %subtract_convert_fusion = bf16[512,4096]{1,0:T(8,128)(2,1)} fusion(bf16[512,4096]{1,0:T(8,128)(2,1)S(1)} %copy-done.2, bf16[512,512]{1,0:T(8,128)(2,1)S(1)} %bitcast.64, bf16[4096,512]{1,0:T(8,128)(2,1)} %param.9), kind=kOutput, calls=%fused_computation | convolution fusion | flops 2155872256 | bytes 13107200 | tf_op jit(solution)/shard_map/dot_general | solution.py:12
  (22 shorter events, 0.4 us)
Async XLA Ops:
  1.6 9.7 %collective-permute-start = (bf16[128,512]{1,0:T(8,128)(2,1)S(1)}, bf16[128,512]{1,0:T(8,128)(2,1)S(1)}, u32[]{:S(2)}, u32[]{:S(2)}) collective-permute-start(bf16[128,512]{1,0:T(8,128)(2,1)S(1)} %get-tuple-element.8), channel_id=1, source_target_pairs={{0,1},{1,2},{2,3},{3,4},{4,5},{5,6},{6,7},{7,0},{8,9},{9,10},{10,1... | collective-permute-start | bytes 393224 | tf_op jit(solution)/shard_map/ppermute | solution.py:29
  4.2 7.2 %collective-permute-start.1 = (bf16[128,512]{1,0:T(8,128)(2,1)S(1)}, bf16[128,512]{1,0:T(8,128)(2,1)S(1)}, u32[]{:S(2)}, u32[]{:S(2)}) collective-permute-start(bf16[128,512]{1,0:T(8,128)(2,1)S(1)} %get-tuple-element.8), channel_id=1, source_target_pairs={{0,7},{1,0},{2,1},{3,2},{4,3},{5,4},{6,5},{7,6},{8,15},{9,8},{10,9... | collective-permute-start | bytes 393224 | tf_op jit(solution)/shard_map/ppermute | solution.py:29
  8.2 5.9 %collective-permute-start.2 = (bf16[128,512]{1,0:T(8,128)(2,1)S(1)}, bf16[128,512]{1,0:T(8,128)(2,1)S(1)}, u32[]{:S(2)}, u32[]{:S(2)}) collective-permute-start(bf16[128,512]{1,0:T(8,128)(2,1)S(1)} %get-tuple-element.7), channel_id=1, source_target_pairs={{0,1},{1,2},{2,3},{3,4},{4,5},{5,6},{6,7},{7,0},{8,9},{9,10},{10,1... | collective-permute-start | bytes 393224 | tf_op jit(solution)/shard_map/ppermute | solution.py:29
  8.2 5.9 %collective-permute-start.3 = (bf16[128,512]{1,0:T(8,128)(2,1)S(1)}, bf16[128,512]{1,0:T(8,128)(2,1)S(1)}, u32[]{:S(2)}, u32[]{:S(2)}) collective-permute-start(bf16[128,512]{1,0:T(8,128)(2,1)S(1)} %get-tuple-element.7), channel_id=1, source_target_pairs={{0,7},{1,0},{2,1},{3,2},{4,3},{5,4},{6,5},{7,6},{8,15},{9,8},{10,9... | collective-permute-start | bytes 393224 | tf_op jit(solution)/shard_map/ppermute | solution.py:29
  11.3 5.5 %collective-permute-start.4 = (bf16[128,512]{1,0:T(8,128)(2,1)S(1)}, bf16[128,512]{1,0:T(8,128)(2,1)S(1)}, u32[]{:S(2)}, u32[]{:S(2)}) collective-permute-start(bf16[128,512]{1,0:T(8,128)(2,1)S(1)} %collective-permute-done), channel_id=1, source_target_pairs={{0,1},{1,2},{2,3},{3,4},{4,5},{5,6},{6,7},{7,0},{8,9},{9,10},{10,1... | collective-permute-start | bytes 393224 | tf_op jit(solution)/shard_map/ppermute | solution.py:29
  11.4 5.5 %collective-permute-start.5 = (bf16[128,512]{1,0:T(8,128)(2,1)S(1)}, bf16[128,512]{1,0:T(8,128)(2,1)S(1)}, u32[]{:S(2)}, u32[]{:S(2)}) collective-permute-start(bf16[128,512]{1,0:T(8,128)(2,1)S(1)} %collective-permute-done.1), channel_id=1, source_target_pairs={{0,7},{1,0},{2,1},{3,2},{4,3},{5,4},{6,5},{7,6},{8,15},{9,8},{10,9... | collective-permute-start | bytes 393224 | tf_op jit(solution)/shard_map/ppermute | solution.py:29
  14.1 5.7 %collective-permute-start.6 = (bf16[128,512]{1,0:T(8,128)(2,1)S(1)}, bf16[128,512]{1,0:T(8,128)(2,1)S(1)}, u32[]{:S(2)}, u32[]{:S(2)}) collective-permute-start(bf16[128,512]{1,0:T(8,128)(2,1)S(1)} %collective-permute-done.2), channel_id=1, source_target_pairs={{0,1},{1,2},{2,3},{3,4},{4,5},{5,6},{6,7},{7,0},{8,9},{9,10},{10,1... | collective-permute-start | bytes 393224 | tf_op jit(solution)/shard_map/ppermute | solution.py:29
  14.1 5.7 %collective-permute-start.7 = (bf16[128,512]{1,0:T(8,128)(2,1)S(1)}, bf16[128,512]{1,0:T(8,128)(2,1)S(1)}, u32[]{:S(2)}, u32[]{:S(2)}) collective-permute-start(bf16[128,512]{1,0:T(8,128)(2,1)S(1)} %collective-permute-done.3), channel_id=1, source_target_pairs={{0,7},{1,0},{2,1},{3,2},{4,3},{5,4},{6,5},{7,6},{8,15},{9,8},{10,9... | collective-permute-start | bytes 393224 | tf_op jit(solution)/shard_map/ppermute | solution.py:29
  16.8 6.2 %collective-permute-start.8 = (bf16[128,512]{1,0:T(8,128)(2,1)S(1)}, bf16[128,512]{1,0:T(8,128)(2,1)S(1)}, u32[]{:S(2)}, u32[]{:S(2)}) collective-permute-start(bf16[128,512]{1,0:T(8,128)(2,1)S(1)} %collective-permute-done.4), channel_id=1, source_target_pairs={{0,1},{1,2},{2,3},{3,4},{4,5},{5,6},{6,7},{7,0},{8,9},{9,10},{10,1... | collective-permute-start | bytes 393224 | tf_op jit(solution)/shard_map/ppermute | solution.py:29
  16.9 11.8 %collective-permute-start.9 = (bf16[128,512]{1,0:T(8,128)(2,1)S(1)}, bf16[128,512]{1,0:T(8,128)(2,1)S(1)}, u32[]{:S(2)}, u32[]{:S(2)}) collective-permute-start(bf16[128,512]{1,0:T(8,128)(2,1)S(1)} %collective-permute-done.5), channel_id=1, source_target_pairs={{0,7},{1,0},{2,1},{3,2},{4,3},{5,4},{6,5},{7,6},{8,15},{9,8},{10,9... | collective-permute-start | bytes 393224 | tf_op jit(solution)/shard_map/ppermute | solution.py:29
  19.8 9.0 %collective-permute-start.10 = (bf16[128,512]{1,0:T(8,128)(2,1)S(1)}, bf16[128,512]{1,0:T(8,128)(2,1)S(1)}, u32[]{:S(2)}, u32[]{:S(2)}) collective-permute-start(bf16[128,512]{1,0:T(8,128)(2,1)S(1)} %collective-permute-done.6), channel_id=1, source_target_pairs={{0,1},{1,2},{2,3},{3,4},{4,5},{5,6},{6,7},{7,0},{8,9},{9,10},{10,1... | collective-permute-start | bytes 393224 | tf_op jit(solution)/shard_map/ppermute | solution.py:29
  19.8 5.6 %collective-permute-start.11 = (bf16[128,512]{1,0:T(8,128)(2,1)S(1)}, bf16[128,512]{1,0:T(8,128)(2,1)S(1)}, u32[]{:S(2)}, u32[]{:S(2)}) collective-permute-start(bf16[128,512]{1,0:T(8,128)(2,1)S(1)} %collective-permute-done.7), channel_id=1, source_target_pairs={{0,7},{1,0},{2,1},{3,2},{4,3},{5,4},{6,5},{7,6},{8,15},{9,8},{10,9... | collective-permute-start | bytes 393224 | tf_op jit(solution)/shard_map/ppermute | solution.py:29
  23.0 5.9 %collective-permute-start.12 = (bf16[128,512]{1,0:T(8,128)(2,1)S(1)}, bf16[128,512]{1,0:T(8,128)(2,1)S(1)}, u32[]{:S(2)}, u32[]{:S(2)}) collective-permute-start(bf16[128,512]{1,0:T(8,128)(2,1)S(1)} %collective-permute-done.8), channel_id=1, source_target_pairs={{0,1},{1,2},{2,3},{3,4},{4,5},{5,6},{6,7},{7,0},{8,9},{9,10},{10,1... | collective-permute-start | bytes 393224 | tf_op jit(solution)/shard_map/ppermute | solution.py:29
  25.3 5.4 %collective-permute-start.13 = (bf16[128,512]{1,0:T(8,128)(2,1)S(1)}, bf16[128,512]{1,0:T(8,128)(2,1)S(1)}, u32[]{:S(2)}, u32[]{:S(2)}) collective-permute-start(bf16[128,512]{1,0:T(8,128)(2,1)S(1)} %collective-permute-done.11), channel_id=1, source_target_pairs={{0,7},{1,0},{2,1},{3,2},{4,3},{5,4},{6,5},{7,6},{8,15},{9,8},{10,9... | collective-permute-start | bytes 393224 | tf_op jit(solution)/shard_map/ppermute | solution.py:29
  30.7 3.6 %copy-start.1 = (bf16[512,4096]{1,0:T(8,128)(2,1)S(1)}, bf16[512,4096]{1,0:T(8,128)(2,1)}, u32[]{:S(2)}) copy-start(bf16[512,4096]{1,0:T(8,128)(2,1)} %param.8) | copy-start | bytes 12582916
  34.3 1.3 %copy-start = (bf16[2,128,512]{2,1,0:T(8,128)(2,1)S(1)}, bf16[2,128,512]{2,1,0:T(8,128)(2,1)}, u32[]{:S(2)}) copy-start(bf16[2,128,512]{2,1,0:T(8,128)(2,1)} %param.7) | copy-start | bytes 786436
  36.9 6.9 %collective-permute-start.14 = (bf16[16,48,512]{2,1,0:T(8,128)(2,1)S(1)}, bf16[16,48,512]{2,1,0:T(8,128)(2,1)S(1)}, u32[]{:S(2)}, u32[]{:S(2)}) collective-permute-start(bf16[16,48,512]{2,1,0:T(8,128)(2,1)S(1)} %dynamic-slice_bitcast_fusion), channel_id=1, source_target_pairs={{0,8},{8,0},{16,24},{24,16},{32,40},{40,32},{48,56},{56,48},{64,72... | collective-permute-start | bytes 2359304 | tf_op jit(solution)/shard_map/ppermute | solution.py:32
  64.5 14.5 %copy-start.3 = (f32[1,16,512]{2,1,0:T(8,128)S(1)}, f32[1,16,512]{2,1,0:T(8,128)}, u32[]{:S(2)}) copy-start(f32[1,16,512]{2,1,0:T(8,128)} %param.11) | copy-start | bytes 98308
  64.5 14.5 %copy-start.4 = (f32[1,16,512]{2,1,0:T(8,128)S(1)}, f32[1,16,512]{2,1,0:T(8,128)}, u32[]{:S(2)}) copy-start(f32[1,16,512]{2,1,0:T(8,128)} %param.10) | copy-start | bytes 98308
  75.4 3.4 %collective-permute-start.15 = (bf16[16,16,512]{2,1,0:T(8,128)(2,1)S(1)}, bf16[16,16,512]{2,1,0:T(8,128)(2,1)S(1)}, u32[]{:S(2)}, u32[]{:S(2)}) collective-permute-start(bf16[16,16,512]{2,1,0:T(8,128)(2,1)S(1)} %all_to_all.16), channel_id=1, source_target_pairs={{0,8},{8,0},{16,24},{24,16},{32,40},{40,32},{48,56},{56,48},{64,72... | collective-permute-start | bytes 786440 | tf_op jit(solution)/shard_map/ppermute | solution.py:32
  79.0 14.6 %copy-start.2 = (bf16[512,4096]{1,0:T(8,128)(2,1)S(1)}, bf16[512,4096]{1,0:T(8,128)(2,1)}, u32[]{:S(2)}) copy-start(bf16[512,4096]{1,0:T(8,128)(2,1)} %param.8) | copy-start | bytes 12582916
  90.7 2.7 %collective-permute-start.16 = (bf16[16,16,512]{2,1,0:T(8,128)(2,1)S(1)}, bf16[16,16,512]{2,1,0:T(8,128)(2,1)S(1)}, u32[]{:S(2)}, u32[]{:S(2)}) collective-permute-start(bf16[16,16,512]{2,1,0:T(8,128)(2,1)S(1)} %all_to_all.17), channel_id=1, source_target_pairs={{0,8},{8,0},{16,24},{24,16},{32,40},{40,32},{48,56},{56,48},{64,72... | collective-permute-start | bytes 786440 | tf_op jit(solution)/shard_map/ppermute | solution.py:32
where the time goes:
time: 100 us
  blocking collectives  42.1 us (42%)
  starting transfers between devices  32.5 us (32%)
  matrix products  13.2 us (13%)
  waiting for transfers between devices  8.78 us (9%)
  local copies, waits for them, and re-layouts  1.64 us (2%)
  between operations  1.15 us (1%)
    all_to_all x3, blocking collectives, exchange(): lax.all_to_all(a, 'dp', split_axis=0, concat_axis=0, tiled=True, axis_ind...  42.1 us
    ppermute x14, starting transfers between devices, ahead(): return lax.ppermute(a, 'mp', [(i, (i + k) % n_mp) for i in range(n_mp)])  23.8 us
    dot_general x7, matrix products, dot(): return lax.dot_general(a, b, (dims, ((), ())), preferred_element_type=F32)  13.2 us
    ppermute x3, starting transfers between devices, other_core(): return lax.ppermute(a, 'dp', [(i, i ^ 1) for i in range(n_dp)])  8.77 us
    ppermute x14, waiting for transfers between devices, ahead(): return lax.ppermute(a, 'mp', [(i, (i + k) % n_mp) for i in range(n_mp)])  4.54 us
    ppermute x3, waiting for transfers between devices, other_core(): return lax.ppermute(a, 'dp', [(i, i ^ 1) for i in range(n_dp)])  4.24 us
  transfers between devices with their start and end apart: 17, of which 8 were waited for; matrix products, arithmetic and copies ran while one was open for 0% of the time, Pallas kernels for 0%

commit v1 on v0

v1 whole, which is shorter than its diff:
```python
import jax
import jax.numpy as jnp
from jax import lax
from jax.sharding import PartitionSpec as P

RATE = 0.02
F32 = jnp.float32
BF16 = jnp.bfloat16


def dot(a, b, dims):
    return lax.dot_general(a, b, (dims, ((), ())), preferred_element_type=F32)


def body(tokens, targets, weight, basis, moment1, moment2):
    n_mp = lax.axis_size("mp")
    n_dp = lax.axis_size("dp")
    j = lax.axis_index("mp")
    core = lax.axis_index("dp") % 2
    chips = n_dp // 2
    steps, toks, width = tokens.shape
    total_tokens = toks * n_dp
    rank = basis.shape[1]
    rows_mp = weight.shape[0]
    rows = rows_mp // n_dp
    groups = [[2 * chip + c for chip in range(chips)] for c in range(2)]

    def ahead(a, k):
        return lax.ppermute(a, "mp", [(i, (i + k) % n_mp) for i in range(n_mp)])

    def other_core(a):
        return lax.ppermute(a, "dp", [(i, i ^ 1) for i in range(n_dp)])

    def exchange(a):
        return lax.all_to_all(a, "dp", split_axis=0, concat_axis=0, tiled=True, axis_index_groups=groups)

    def pair_rows(parts):
        away = other_core(lax.dynamic_index_in_dim(parts, 1 - core, 1, keepdims=False))
        kept = lax.dynamic_index_in_dim(parts, core, 1, keepdims=False)
        return (kept.astype(F32) + away.astype(F32)).astype(BF16)

    def by_owner(a, b):
        return dot(a, b, ((0,), (0,))).astype(BF16).reshape(chips, 2, -1, rank)

    def both_cores(mine):
        other = other_core(mine)
        both = [jnp.where(core == 0, mine, other), jnp.where(core == 0, other, mine)]
        return jnp.stack(both, axis=1).reshape(-1, mine.shape[-1])

    def for_each_chip(a):
        return jnp.broadcast_to(a, (chips, *a.shape))

    half = n_mp // 2
    own = lax.optimization_barrier([tokens[s] for s in range(steps)])
    right, left = list(own), list(own)

    def put(features, chunk, k):
        return lax.dynamic_update_slice(features, chunk, (0, ((j - k) % n_mp) * width))

    features = [put(jnp.zeros((toks, n_mp * width), BF16), own[s], 0) for s in range(steps)]
    for k in range(1, half):
        for s in (1, 0):
            right[s] = ahead(right[s], 1)
            left[s] = ahead(left[s], -1)
            features[s] = put(put(features[s], right[s], k), left[s], -k)
    last1 = ahead(right[1], 1)
    last0 = ahead(left[0], -1)

    features[1] = put(features[1], last1, half)
    reduced1 = lax.optimization_barrier(dot(features[1], basis, ((1,), (0,))).astype(BF16))
    gram_parts = by_owner(reduced1, reduced1)
    gram_parts, last0, features[1] = lax.optimization_barrier((gram_parts, last0, features[1]))
    features[0] = put(features[0], last0, half)
    reduced0 = lax.optimization_barrier(dot(features[0], basis, ((1,), (0,))).astype(BF16))
    pair = pair_rows(gram_parts)
    arrived = exchange(pair)
    gram_rows = arrived.astype(F32).sum(axis=0).astype(BF16)

    reduced = [reduced0, reduced1]
    outputs = [dot(features[s], weight, ((1,), (1,))) for s in range(steps)]
    outputs = lax.optimization_barrier(outputs)
    errors = [(outputs[s].astype(BF16).astype(F32) - targets[s].astype(F32)).astype(BF16) for s in range(steps)]
    parts = jnp.concatenate([by_owner(errors[s], reduced[s]) for s in range(steps)], axis=2)
    pair = pair_rows(parts)
    arrived = exchange(jnp.concatenate([pair, for_each_chip(gram_rows)], axis=1))
    sums = arrived[:, : steps * rows].astype(F32).sum(axis=0)
    gram = both_cores(arrived[:, steps * rows :])

    def update(first, second, projected):
        first = 0.9 * first + 0.1 * projected
        second = 0.95 * second + 0.05 * projected * projected
        direction = (first / (jnp.sqrt(second) + 1e-08)).astype(BF16)
        return first, second, direction

    first, second, d0 = update(moment1[0], moment2[0], sums[:rows] / total_tokens)
    moved = dot(d0, gram, ((1,), (0,)))
    first, second, d1 = update(first, second, (sums[rows:] - RATE * moved) / total_tokens)
    both = (d0.astype(F32) + d1.astype(F32)).astype(BF16)
    lifted = dot(both_cores(exchange(for_each_chip(both))), basis, ((1,), (1,)))
    new_weight = (weight.astype(F32) - RATE * lifted).astype(BF16)
    return (new_weight, first[None], second[None])


def solution(mesh):
    in_specs = (
        P(None, "dp", "mp"),
        P(None, "dp", "mp"),
        P("mp", None),
        P(),
        P("mp", "dp", None),
        P("mp", "dp", None),
    )
    out_specs = (P("mp", None), P("mp", "dp", None), P("mp", "dp", None))
    return jax.shard_map(body, mesh=mesh, in_specs=in_specs, out_specs=out_specs, check_vma=False)
```

time: 100 us -> 102 us (1.020)
  waiting for transfers between devices: 8.78 us -> 10.8 us
  blocking collectives: 42.1 us -> 40.7 us
  local copies, waits for them, and re-layouts: 1.64 us -> 2.67 us
    ppermute x14, waiting for transfers between devices: 4.54 us -> 8.19 us  [ahead(): return lax.ppermute(a, 'mp', [(i, (i + k) % n_mp) for i in range(n_mp)])]
    ppermute x3 -> x4, waiting for transfers between devices: 4.24 us -> 2.58 us  [other_core(): return lax.ppermute(a, 'dp', [(i, i ^ 1) for i in range(n_dp)])]
    all_to_all x3, blocking collectives: 42.1 us -> 40.7 us  [exchange(): lax.all_to_all(a, 'dp', split_axis=0, concat_axis=0, tiled=True, axis_ind...]
    unnamed x10 -> x12, local copies, waits for them, and re-layouts: 0.03 us -> 1.12 us
    ppermute x3 -> x4, starting transfers between devices: 8.77 us -> 9.75 us  [other_core(): return lax.ppermute(a, 'dp', [(i, i ^ 1) for i in range(n_dp)])]
    dot_general x7 -> x9, matrix products: 13.2 us -> 12.9 us  [dot(): return lax.dot_general(a, b, (dims, ((), ())), preferred_element_type=F32)]
  transfers between devices with their start and end apart: 17 -> 18, of which waited for: 8 -> 6; matrix products, arithmetic and copies ran while one was open for 0% -> 2% of each run, Pallas kernels for 0% -> 0%
where the time goes in v1:
time: 102 us
  blocking collectives  40.7 us (40%)
  starting transfers between devices  33.2 us (33%)
  matrix products  12.9 us (13%)
  waiting for transfers between devices  10.8 us (11%)
  local copies, waits for them, and re-layouts  2.67 us (3%)
  between operations  1.21 us (1%)
    all_to_all x3, blocking collectives, exchange(): lax.all_to_all(a, 'dp', split_axis=0, concat_axis=0, tiled=True, axis_ind...  40.7 us
    ppermute x14, starting transfers between devices, ahead(): return lax.ppermute(a, 'mp', [(i, (i + k) % n_mp) for i in range(n_mp)])  23.4 us
    dot_general x9, matrix products, dot(): return lax.dot_general(a, b, (dims, ((), ())), preferred_element_type=F32)  12.9 us
    ppermute x4, starting transfers between devices, other_core(): return lax.ppermute(a, 'dp', [(i, i ^ 1) for i in range(n_dp)])  9.75 us
    ppermute x14, waiting for transfers between devices, ahead(): return lax.ppermute(a, 'mp', [(i, (i + k) % n_mp) for i in range(n_mp)])  8.19 us
    ppermute x4, waiting for transfers between devices, other_core(): return lax.ppermute(a, 'dp', [(i, i ^ 1) for i in range(n_dp)])  2.58 us
  transfers between devices with their start and end apart: 18, of which 6 were waited for; matrix products, arithmetic and copies ran while one was open for 2% of the time, Pallas kernels for 0%

profile of v1, /device:TPU:1, one launch (start us, length us, event | category | flops | bytes accessed | tf_op | source)
XLA Modules:
  0.0 102.1 jit_solution(2296255030386092711)
XLA Ops:
  0.6 1.0 slice_bitcast_fusion
  1.6 6.5 %collective-permute-start.1 = (bf16[128,512]{1,0:T(8,128)(2,1)S(1)}, bf16[128,512]{1,0:T(8,128)(2,1)S(1)}, u32[]{:S(2)}, u32[]{:S(2)}) collective-permute-start(bf16[128,512]{1,0:T(8,128)(2,1)S(1)} %get-tuple-element.10), channel_id=1, source_target_pairs={{0,7},{1,0},{2,1},{3,2},{4,3},{5,4},{6,5},{7,6},{8,15},{9,8},{10,9... | collective-permute-start | bytes 393224 | tf_op jit(solution)/shard_map/ppermute | solution.py:29
  8.1 0.0 collective-permute-start
  8.1 2.7 %collective-permute-start.7 = (bf16[128,512]{1,0:T(8,128)(2,1)S(1)}, bf16[128,512]{1,0:T(8,128)(2,1)S(1)}, u32[]{:S(2)}, u32[]{:S(2)}) collective-permute-start(bf16[128,512]{1,0:T(8,128)(2,1)S(1)} %get-tuple-element.11), channel_id=1, source_target_pairs={{0,7},{1,0},{2,1},{3,2},{4,3},{5,4},{6,5},{7,6},{8,15},{9,8},{10,9... | collective-permute-start | bytes 393224 | tf_op jit(solution)/shard_map/ppermute | solution.py:29
  10.8 0.0 collective-permute-start.6
  10.8 0.1 broadcast.41.clone
  11.0 0.0 copy-start.2
  11.1 0.1 broadcast.41.clone.1
  11.2 0.0 collective-permute-done.1
  11.2 2.7 %collective-permute-start.3 = (bf16[128,512]{1,0:T(8,128)(2,1)S(1)}, bf16[128,512]{1,0:T(8,128)(2,1)S(1)}, u32[]{:S(2)}, u32[]{:S(2)}) collective-permute-start(bf16[128,512]{1,0:T(8,128)(2,1)S(1)} %collective-permute-done.1), channel_id=1, source_target_pairs={{0,7},{1,0},{2,1},{3,2},{4,3},{5,4},{6,5},{7,6},{8,15},{9,8},{10,9... | collective-permute-start | bytes 393224 | tf_op jit(solution)/shard_map/ppermute | solution.py:29
  13.9 0.0 collective-permute-done
  13.9 0.0 collective-permute-start.2
  14.0 0.0 collective-permute-done.7
  14.0 2.7 %collective-permute-start.9 = (bf16[128,512]{1,0:T(8,128)(2,1)S(1)}, bf16[128,512]{1,0:T(8,128)(2,1)S(1)}, u32[]{:S(2)}, u32[]{:S(2)}) collective-permute-start(bf16[128,512]{1,0:T(8,128)(2,1)S(1)} %collective-permute-done.7), channel_id=1, source_target_pairs={{0,7},{1,0},{2,1},{3,2},{4,3},{5,4},{6,5},{7,6},{8,15},{9,8},{10,9... | collective-permute-start | bytes 393224 | tf_op jit(solution)/shard_map/ppermute | solution.py:29
  16.6 0.0 collective-permute-done.6
  16.6 0.0 collective-permute-start.8
  16.7 0.0 collective-permute-done.3
  16.7 2.7 %collective-permute-start.5 = (bf16[128,512]{1,0:T(8,128)(2,1)S(1)}, bf16[128,512]{1,0:T(8,128)(2,1)S(1)}, u32[]{:S(2)}, u32[]{:S(2)}) collective-permute-start(bf16[128,512]{1,0:T(8,128)(2,1)S(1)} %collective-permute-done.3), channel_id=1, source_target_pairs={{0,7},{1,0},{2,1},{3,2},{4,3},{5,4},{6,5},{7,6},{8,15},{9,8},{10,9... | collective-permute-start | bytes 393224 | tf_op jit(solution)/shard_map/ppermute | solution.py:29
  19.5 0.0 collective-permute-done.2
  19.5 0.0 collective-permute-start.4
  19.5 0.0 collective-permute-done.9
  19.5 3.1 %collective-permute-start.11 = (bf16[128,512]{1,0:T(8,128)(2,1)S(1)}, bf16[128,512]{1,0:T(8,128)(2,1)S(1)}, u32[]{:S(2)}, u32[]{:S(2)}) collective-permute-start(bf16[128,512]{1,0:T(8,128)(2,1)S(1)} %collective-permute-done.9), channel_id=1, source_target_pairs={{0,7},{1,0},{2,1},{3,2},{4,3},{5,4},{6,5},{7,6},{8,15},{9,8},{10,9... | collective-permute-start | bytes 393224 | tf_op jit(solution)/shard_map/ppermute | solution.py:29
  22.6 0.4 collective-permute-done.8
  23.1 0.0 collective-permute-start.10
  23.2 0.0 collective-permute-done.5
  23.2 3.0 %collective-permute-start.13 = (bf16[128,512]{1,0:T(8,128)(2,1)S(1)}, bf16[128,512]{1,0:T(8,128)(2,1)S(1)}, u32[]{:S(2)}, u32[]{:S(2)}) collective-permute-start(bf16[128,512]{1,0:T(8,128)(2,1)S(1)} %collective-permute-done.5), channel_id=1, source_target_pairs={{0,7},{1,0},{2,1},{3,2},{4,3},{5,4},{6,5},{7,6},{8,15},{9,8},{10,9... | collective-permute-start | bytes 393224 | tf_op jit(solution)/shard_map/ppermute | solution.py:29
  26.1 2.8 %collective-permute-done.10 = bf16[128,512]{1,0:T(8,128)(2,1)S(1)} collective-permute-done((bf16[128,512]{1,0:T(8,128)(2,1)S(1)}, bf16[128,512]{1,0:T(8,128)(2,1)S(1)}, u32[]{:S(2)}, u32[]{:S(2)}) %collective-permute-start.10) | collective-permute-done | bytes 131104 | tf_op jit(solution)/shard_map/ppermute | solution.py:29
  28.9 0.0 collective-permute-start.12
  29.0 0.0 collective-permute-done.4
  29.0 0.0 collective-permute-done.11
  29.0 4.9 %collective-permute-done.12 = bf16[128,512]{1,0:T(8,128)(2,1)S(1)} collective-permute-done((bf16[128,512]{1,0:T(8,128)(2,1)S(1)}, bf16[128,512]{1,0:T(8,128)(2,1)S(1)}, u32[]{:S(2)}, u32[]{:S(2)}) %collective-permute-start.12) | collective-permute-done | bytes 131104 | tf_op jit(solution)/shard_map/ppermute | solution.py:29
  34.0 0.8 convolution_convert_fusion.4
  34.8 0.0 copy-start
  34.8 0.3 convolution_convert_fusion.2
  35.1 0.0 collective-permute-done.13
  35.1 0.7 convolution_convert_fusion.3
  35.9 1.1 %copy-done = bf16[512,4096]{1,0:T(8,128)(2,1)S(1)} copy-done((bf16[512,4096]{1,0:T(8,128)(2,1)S(1)}, bf16[512,4096]{1,0:T(8,128)(2,1)}, u32[]{:S(2)}) %copy-start) | copy-done | bytes 4194328
  37.0 1.5 %fusion.19 = bf16[128,512]{1,0:T(8,128)(2,1)S(1)} fusion(bf16[128,4096]{1,0:T(8,128)(2,1)S(1)} %constant_dynamic-update-slice_fusion, bf16[512,4096]{1,0:T(8,128)(2,1)S(1)} %copy-done), kind=kOutput, calls=%fused_computation.66 | convolution fusion | flops 536870912 | bytes 5373952 | tf_op jit(solution)/shard_map/dot_general | solution.py:12
  38.5 0.0 copy-start.3
  38.5 1.5 %fusion.20 = bf16[128,512]{1,0:T(8,128)(2,1)S(1)} fusion(bf16[128,4096]{1,0:T(8,128)(2,1)S(1)} %constant_dynamic-update-slice_fusion.1, bf16[512,4096]{1,0:T(8,128)(2,1)S(1)} %copy-done), kind=kOutput, calls=%fused_computation.67 | convolution fusion | flops 536870912 | bytes 5373952 | tf_op jit(solution)/shard_map/dot_general | solution.py:12
  40.1 5.3 %collective-permute-start.15 = (bf16[16,16,512]{2,1,0:T(8,128)(2,1)S(1)}, bf16[16,16,512]{2,1,0:T(8,128)(2,1)S(1)}, u32[]{:S(2)}, u32[]{:S(2)}) collective-permute-start(bf16[16,16,512]{2,1,0:T(8,128)(2,1)S(1)} %dynamic-slice_bitcast_fusion), channel_id=1, source_target_pairs={{0,8},{8,0},{16,24},{24,16},{32,40},{40,32},{48,56},{56,48},{64,72... | collective-permute-start | bytes 786440 | tf_op jit(solution)/shard_map/ppermute | solution.py:32
  45.4 0.3 convolution_convert_fusion
  45.7 0.3 convolution_convert_fusion.1
  46.0 0.1 fusion.3
  46.1 0.1 collective-permute-start.14
  46.2 0.3 collective-permute-done.15
  46.5 0.1 fusion.6
  46.6 14.7 %all_to_all.17 = bf16[16,16,512]{2,1,0:T(8,128)(2,1)S(1)} all-to-all(bf16[16,16,512]{2,1,0:T(8,128)(2,1)S(1)} %fusion.6), channel_id=1, replica_groups={{0,16,32,48,64,80,96,112,128,144,160,176,192,208,224,240},{8,24,40,56,7..., dimensions={0} | all-to-all | bytes 524288 | tf_op jit(solution)/shard_map/all_to_all | solution.py:35
  61.4 0.0 copy-start.4
  61.4 0.0 copy-start.5
  61.4 0.0 collective-permute-done.14
  61.4 0.2 fusion.1
  61.6 0.1 pad_maximum_fusion
  61.6 15.2 %all_to_all.15 = bf16[16,48,512]{2,1,0:T(8,128)(2,1)S(1)} all-to-all(bf16[16,48,512]{2,1,0:T(8,128)(2,1)S(1)} %pad_maximum_fusion), channel_id=1, replica_groups={{0,16,32,48,64,80,96,112,128,144,160,176,192,208,224,240},{8,24,40,56,7..., dimensions={0} | all-to-all | bytes 1572864 | tf_op jit(solution)/shard_map/all_to_all | solution.py:35
  76.9 2.8 %collective-permute-start.16 = (bf16[16,16,512]{2,1,0:T(8,128)(2,1)S(1)}, bf16[16,16,512]{2,1,0:T(8,128)(2,1)S(1)}, u32[]{:S(2)}, u32[]{:S(2)}) collective-permute-start(bf16[16,16,512]{2,1,0:T(8,128)(2,1)S(1)} %slice.35), channel_id=1, source_target_pairs={{0,8},{8,0},{16,24},{24,16},{32,40},{40,32},{48,56},{56,48},{64,72... | collective-permute-start | bytes 786440 | tf_op jit(solution)/shard_map/ppermute | solution.py:32
  79.8 0.1 convert_reduce_fusion
  79.8 1.1 %collective-permute-done.16 = bf16[16,16,512]{2,1,0:T(8,128)(2,1)S(1)} collective-permute-done((bf16[16,16,512]{2,1,0:T(8,128)(2,1)S(1)}, bf16[16,16,512]{2,1,0:T(8,128)(2,1)S(1)}, u32[]{:S(2)}, u32[]{:S(2)}) %collective-permute-start.16) | collective-permute-done | bytes 262176 | tf_op jit(solution)/shard_map/ppermute | solution.py:32
  81.0 0.1 pad_maximum_fusion.1
  81.0 0.8 fusion.18
  81.9 10.8 %all_to_all.16 = bf16[16,16,512]{2,1,0:T(8,128)(2,1)S(1)} all-to-all(bf16[16,16,512]{2,1,0:T(8,128)(2,1)S(1)} %broadcast_in_dim.13), channel_id=1, replica_groups={{0,16,32,48,64,80,96,112,128,144,160,176,192,208,224,240},{8,24,40,56,7..., dimensions={0} | all-to-all | bytes 524288 | tf_op jit(solution)/shard_map/all_to_all | solution.py:35
  92.7 1.5 %collective-permute-start.17 = (bf16[16,16,512]{2,1,0:T(8,128)(2,1)S(1)}, bf16[16,16,512]{2,1,0:T(8,128)(2,1)S(1)}, u32[]{:S(2)}, u32[]{:S(2)}) collective-permute-start(bf16[16,16,512]{2,1,0:T(8,128)(2,1)S(1)} %all_to_all.16), channel_id=1, source_target_pairs={{0,8},{8,0},{16,24},{24,16},{32,40},{40,32},{48,56},{56,48},{64,72... | collective-permute-start | bytes 786440 | tf_op jit(solution)/shard_map/ppermute | solution.py:32
  94.2 1.2 %collective-permute-done.17 = bf16[16,16,512]{2,1,0:T(8,128)(2,1)S(1)} collective-permute-done((bf16[16,16,512]{2,1,0:T(8,128)(2,1)S(1)}, bf16[16,16,512]{2,1,0:T(8,128)(2,1)S(1)}, u32[]{:S(2)}, u32[]{:S(2)}) %collective-permute-start.17) | collective-permute-done | bytes 262176 | tf_op jit(solution)/shard_map/ppermute | solution.py:32
  95.4 0.1 pad_maximum_fusion.2
  95.5 6.6 %subtract_convert_fusion = bf16[512,4096]{1,0:T(8,128)(2,1)} fusion(bf16[512,4096]{1,0:T(8,128)(2,1)S(1)} %copy-done.1, bf16[512,512]{1,0:T(8,128)(2,1)S(1)} %bitcast.95, bf16[4096,512]{1,0:T(8,128)(2,1)} %param.9), kind=kOutput, calls=%fused_computation | convolution fusion | flops 2155872256 | bytes 13107200 | tf_op jit(solution)/shard_map/dot_general | solution.py:12
  (30 shorter events, 0.5 us)
Async XLA Ops:
  1.6 9.6 %collective-permute-start.1 = (bf16[128,512]{1,0:T(8,128)(2,1)S(1)}, bf16[128,512]{1,0:T(8,128)(2,1)S(1)}, u32[]{:S(2)}, u32[]{:S(2)}) collective-permute-start(bf16[128,512]{1,0:T(8,128)(2,1)S(1)} %get-tuple-element.10), channel_id=1, source_target_pairs={{0,7},{1,0},{2,1},{3,2},{4,3},{5,4},{6,5},{7,6},{8,15},{9,8},{10,9... | collective-permute-start | bytes 393224 | tf_op jit(solution)/shard_map/ppermute | solution.py:29
  8.1 5.9 %collective-permute-start = (bf16[128,512]{1,0:T(8,128)(2,1)S(1)}, bf16[128,512]{1,0:T(8,128)(2,1)S(1)}, u32[]{:S(2)}, u32[]{:S(2)}) collective-permute-start(bf16[128,512]{1,0:T(8,128)(2,1)S(1)} %get-tuple-element.10), channel_id=1, source_target_pairs={{0,1},{1,2},{2,3},{3,4},{4,5},{5,6},{6,7},{7,0},{8,9},{9,10},{10,1... | collective-permute-start | bytes 393224 | tf_op jit(solution)/shard_map/ppermute | solution.py:29
  8.1 5.9 %collective-permute-start.7 = (bf16[128,512]{1,0:T(8,128)(2,1)S(1)}, bf16[128,512]{1,0:T(8,128)(2,1)S(1)}, u32[]{:S(2)}, u32[]{:S(2)}) collective-permute-start(bf16[128,512]{1,0:T(8,128)(2,1)S(1)} %get-tuple-element.11), channel_id=1, source_target_pairs={{0,7},{1,0},{2,1},{3,2},{4,3},{5,4},{6,5},{7,6},{8,15},{9,8},{10,9... | collective-permute-start | bytes 393224 | tf_op jit(solution)/shard_map/ppermute | solution.py:29
  10.8 5.9 %collective-permute-start.6 = (bf16[128,512]{1,0:T(8,128)(2,1)S(1)}, bf16[128,512]{1,0:T(8,128)(2,1)S(1)}, u32[]{:S(2)}, u32[]{:S(2)}) collective-permute-start(bf16[128,512]{1,0:T(8,128)(2,1)S(1)} %get-tuple-element.11), channel_id=1, source_target_pairs={{0,1},{1,2},{2,3},{3,4},{4,5},{5,6},{6,7},{7,0},{8,9},{9,10},{10,1... | collective-permute-start | bytes 393224 | tf_op jit(solution)/shard_map/ppermute | solution.py:29
  11.0 22.9 %copy-start.2 = (bf16[4096,512]{1,0:T(8,128)(2,1)S(1)}, bf16[4096,512]{1,0:T(8,128)(2,1)}, u32[]{:S(2)}) copy-start(bf16[4096,512]{1,0:T(8,128)(2,1)} %param.9) | copy-start | bytes 12582916
  11.2 5.5 %collective-permute-start.3 = (bf16[128,512]{1,0:T(8,128)(2,1)S(1)}, bf16[128,512]{1,0:T(8,128)(2,1)S(1)}, u32[]{:S(2)}, u32[]{:S(2)}) collective-permute-start(bf16[128,512]{1,0:T(8,128)(2,1)S(1)} %collective-permute-done.1), channel_id=1, source_target_pairs={{0,7},{1,0},{2,1},{3,2},{4,3},{5,4},{6,5},{7,6},{8,15},{9,8},{10,9... | collective-permute-start | bytes 393224 | tf_op jit(solution)/shard_map/ppermute | solution.py:29
  13.9 5.5 %collective-permute-start.2 = (bf16[128,512]{1,0:T(8,128)(2,1)S(1)}, bf16[128,512]{1,0:T(8,128)(2,1)S(1)}, u32[]{:S(2)}, u32[]{:S(2)}) collective-permute-start(bf16[128,512]{1,0:T(8,128)(2,1)S(1)} %collective-permute-done), channel_id=1, source_target_pairs={{0,1},{1,2},{2,3},{3,4},{4,5},{5,6},{6,7},{7,0},{8,9},{9,10},{10,1... | collective-permute-start | bytes 393224 | tf_op jit(solution)/shard_map/ppermute | solution.py:29
  14.0 5.6 %collective-permute-start.9 = (bf16[128,512]{1,0:T(8,128)(2,1)S(1)}, bf16[128,512]{1,0:T(8,128)(2,1)S(1)}, u32[]{:S(2)}, u32[]{:S(2)}) collective-permute-start(bf16[128,512]{1,0:T(8,128)(2,1)S(1)} %collective-permute-done.7), channel_id=1, source_target_pairs={{0,7},{1,0},{2,1},{3,2},{4,3},{5,4},{6,5},{7,6},{8,15},{9,8},{10,9... | collective-permute-start | bytes 393224 | tf_op jit(solution)/shard_map/ppermute | solution.py:29
  16.6 6.4 %collective-permute-start.8 = (bf16[128,512]{1,0:T(8,128)(2,1)S(1)}, bf16[128,512]{1,0:T(8,128)(2,1)S(1)}, u32[]{:S(2)}, u32[]{:S(2)}) collective-permute-start(bf16[128,512]{1,0:T(8,128)(2,1)S(1)} %collective-permute-done.6), channel_id=1, source_target_pairs={{0,1},{1,2},{2,3},{3,4},{4,5},{5,6},{6,7},{7,0},{8,9},{9,10},{10,1... | collective-permute-start | bytes 393224 | tf_op jit(solution)/shard_map/ppermute | solution.py:29
  16.7 6.4 %collective-permute-start.5 = (bf16[128,512]{1,0:T(8,128)(2,1)S(1)}, bf16[128,512]{1,0:T(8,128)(2,1)S(1)}, u32[]{:S(2)}, u32[]{:S(2)}) collective-permute-start(bf16[128,512]{1,0:T(8,128)(2,1)S(1)} %collective-permute-done.3), channel_id=1, source_target_pairs={{0,7},{1,0},{2,1},{3,2},{4,3},{5,4},{6,5},{7,6},{8,15},{9,8},{10,9... | collective-permute-start | bytes 393224 | tf_op jit(solution)/shard_map/ppermute | solution.py:29
  19.5 9.5 %collective-permute-start.4 = (bf16[128,512]{1,0:T(8,128)(2,1)S(1)}, bf16[128,512]{1,0:T(8,128)(2,1)S(1)}, u32[]{:S(2)}, u32[]{:S(2)}) collective-permute-start(bf16[128,512]{1,0:T(8,128)(2,1)S(1)} %collective-permute-done.2), channel_id=1, source_target_pairs={{0,1},{1,2},{2,3},{3,4},{4,5},{5,6},{6,7},{7,0},{8,9},{9,10},{10,1... | collective-permute-start | bytes 393224 | tf_op jit(solution)/shard_map/ppermute | solution.py:29
  19.5 9.5 %collective-permute-start.11 = (bf16[128,512]{1,0:T(8,128)(2,1)S(1)}, bf16[128,512]{1,0:T(8,128)(2,1)S(1)}, u32[]{:S(2)}, u32[]{:S(2)}) collective-permute-start(bf16[128,512]{1,0:T(8,128)(2,1)S(1)} %collective-permute-done.9), channel_id=1, source_target_pairs={{0,7},{1,0},{2,1},{3,2},{4,3},{5,4},{6,5},{7,6},{8,15},{9,8},{10,9... | collective-permute-start | bytes 393224 | tf_op jit(solution)/shard_map/ppermute | solution.py:29
  23.1 5.9 %collective-permute-start.10 = (bf16[128,512]{1,0:T(8,128)(2,1)S(1)}, bf16[128,512]{1,0:T(8,128)(2,1)S(1)}, u32[]{:S(2)}, u32[]{:S(2)}) collective-permute-start(bf16[128,512]{1,0:T(8,128)(2,1)S(1)} %collective-permute-done.8), channel_id=1, source_target_pairs={{0,1},{1,2},{2,3},{3,4},{4,5},{5,6},{6,7},{7,0},{8,9},{9,10},{10,1... | collective-permute-start | bytes 393224 | tf_op jit(solution)/shard_map/ppermute | solution.py:29
  23.2 11.9 %collective-permute-start.13 = (bf16[128,512]{1,0:T(8,128)(2,1)S(1)}, bf16[128,512]{1,0:T(8,128)(2,1)S(1)}, u32[]{:S(2)}, u32[]{:S(2)}) collective-permute-start(bf16[128,512]{1,0:T(8,128)(2,1)S(1)} %collective-permute-done.5), channel_id=1, source_target_pairs={{0,7},{1,0},{2,1},{3,2},{4,3},{5,4},{6,5},{7,6},{8,15},{9,8},{10,9... | collective-permute-start | bytes 393224 | tf_op jit(solution)/shard_map/ppermute | solution.py:29
  28.9 5.0 %collective-permute-start.12 = (bf16[128,512]{1,0:T(8,128)(2,1)S(1)}, bf16[128,512]{1,0:T(8,128)(2,1)S(1)}, u32[]{:S(2)}, u32[]{:S(2)}) collective-permute-start(bf16[128,512]{1,0:T(8,128)(2,1)S(1)} %collective-permute-done.10), channel_id=1, source_target_pairs={{0,1},{1,2},{2,3},{3,4},{4,5},{5,6},{6,7},{7,0},{8,9},{9,10},{10,1... | collective-permute-start | bytes 393224 | tf_op jit(solution)/shard_map/ppermute | solution.py:29
  34.8 2.2 %copy-start = (bf16[512,4096]{1,0:T(8,128)(2,1)S(1)}, bf16[512,4096]{1,0:T(8,128)(2,1)}, u32[]{:S(2)}) copy-start(bf16[512,4096]{1,0:T(8,128)(2,1)} %param.8) | copy-start | bytes 12582916
  38.5 6.9 %copy-start.3 = (bf16[2,128,512]{2,1,0:T(8,128)(2,1)S(1)}, bf16[2,128,512]{2,1,0:T(8,128)(2,1)}, u32[]{:S(2)}) copy-start(bf16[2,128,512]{2,1,0:T(8,128)(2,1)} %param.7) | copy-start | bytes 786436
  40.1 6.5 %collective-permute-start.15 = (bf16[16,16,512]{2,1,0:T(8,128)(2,1)S(1)}, bf16[16,16,512]{2,1,0:T(8,128)(2,1)S(1)}, u32[]{:S(2)}, u32[]{:S(2)}) collective-permute-start(bf16[16,16,512]{2,1,0:T(8,128)(2,1)S(1)} %dynamic-slice_bitcast_fusion), channel_id=1, source_target_pairs={{0,8},{8,0},{16,24},{24,16},{32,40},{40,32},{48,56},{56,48},{64,72... | collective-permute-start | bytes 786440 | tf_op jit(solution)/shard_map/ppermute | solution.py:32
  46.1 15.3 %collective-permute-start.14 = (bf16[16,32,512]{2,1,0:T(8,128)(2,1)S(1)}, bf16[16,32,512]{2,1,0:T(8,128)(2,1)S(1)}, u32[]{:S(2)}, u32[]{:S(2)}) collective-permute-start(bf16[16,32,512]{2,1,0:T(8,128)(2,1)S(1)} %fusion.3), channel_id=1, source_target_pairs={{0,8},{8,0},{16,24},{24,16},{32,40},{40,32},{48,56},{56,48},{64,72... | collective-permute-start | bytes 1572872 | tf_op jit(solution)/shard_map/ppermute | solution.py:32
  61.4 19.7 %copy-start.4 = (f32[1,16,512]{2,1,0:T(8,128)S(1)}, f32[1,16,512]{2,1,0:T(8,128)}, u32[]{:S(2)}) copy-start(f32[1,16,512]{2,1,0:T(8,128)} %param.11) | copy-start | bytes 98308
  61.4 19.7 %copy-start.5 = (f32[1,16,512]{2,1,0:T(8,128)S(1)}, f32[1,16,512]{2,1,0:T(8,128)}, u32[]{:S(2)}) copy-start(f32[1,16,512]{2,1,0:T(8,128)} %param.10) | copy-start | bytes 98308
  76.9 4.0 %collective-permute-start.16 = (bf16[16,16,512]{2,1,0:T(8,128)(2,1)S(1)}, bf16[16,16,512]{2,1,0:T(8,128)(2,1)S(1)}, u32[]{:S(2)}, u32[]{:S(2)}) collective-permute-start(bf16[16,16,512]{2,1,0:T(8,128)(2,1)S(1)} %slice.35), channel_id=1, source_target_pairs={{0,8},{8,0},{16,24},{24,16},{32,40},{40,32},{48,56},{56,48},{64,72... | collective-permute-start | bytes 786440 | tf_op jit(solution)/shard_map/ppermute | solution.py:32
  79.8 15.8 %copy-start.1 = (bf16[512,4096]{1,0:T(8,128)(2,1)S(1)}, bf16[512,4096]{1,0:T(8,128)(2,1)}, u32[]{:S(2)}) copy-start(bf16[512,4096]{1,0:T(8,128)(2,1)} %param.8) | copy-start | bytes 12582916
  92.7 2.7 %collective-permute-start.17 = (bf16[16,16,512]{2,1,0:T(8,128)(2,1)S(1)}, bf16[16,16,512]{2,1,0:T(8,128)(2,1)S(1)}, u32[]{:S(2)}, u32[]{:S(2)}) collective-permute-start(bf16[16,16,512]{2,1,0:T(8,128)(2,1)S(1)} %all_to_all.16), channel_id=1, source_target_pairs={{0,8},{8,0},{16,24},{24,16},{32,40},{40,32},{48,56},{56,48},{64,72... | collective-permute-start | bytes 786440 | tf_op jit(solution)/shard_map/ppermute | solution.py:32
